TPU v7x, 768 devices: a whole 4x8x12 slice. The times are simulated.
768 devices in a mesh: dp: 24 (over x, z_hi, core), tensor: 32 (over y, z_lo).
Axes of the slice: x: 4, y: 8, z: 12 (z_hi: 3, z_lo: 4; z = z_hi * 4 + z_lo), core: 2. Of those that a mesh axis runs over, the one named last changes fastest.
Arguments:
- queries: bfloat16 [24, 4, 64, 8192], P('dp', None, None, 'tensor'), may hold values from -64 to 64
- slot_keys_values: bfloat16 [24, 4, 2, 64, 1024], P('dp'), may hold values from -8 to 8
- segment_ids: int32 [24, 4, 64], P('dp'), may hold values from 0 to 3, never falling along the last dimension, each value on 1 to 32 neighbouring positions
- residual_in: bfloat16 [24, 4, 64, 4224], P('dp', None, None, 'tensor'), may hold values from -6 to 6
- cotangent: bfloat16 [24, 4, 64, 4224], P('dp', None, None, 'tensor'), may hold values from -192 to 192
- out_weight: bfloat16 [8192, 4224], P('tensor', 'dp'), may hold values from -0.0625 to 0.0625
- live_mask: int32 [24], replicated, may hold values 0 or 1
- micro_counts: int32 [24], replicated, may hold values from 1 to 4
Outputs:
- block_residual: bfloat16 [24, 4, 64, 4224], P('dp', None, None, 'tensor')
- query_gradient: bfloat16 [24, 4, 64, 8192], P('dp', None, None, 'tensor')
- key_value_grad: bfloat16 [24, 4, 2, 64, 1024], P('dp')
- projection_weight_gradient: float32 [8192, 4224], P('tensor', 'dp')
All inputs are finite; a program needn't handle non-finite values.
Results may differ from a plain program's by a relative error of at most 0.014.
Values may be sent and summed in bfloat16 or wider, within the bound.
A program may use at most 64 MiB of HBM per device.

v0:
```python
import math

import jax
import jax.numpy as jnp
from jax import lax
from jax.sharding import PartitionSpec as P

HEAD_SIZE = 128
QUERY_HEADS = 64
KEY_VALUE_HEADS = 8


def attention_backward(query_f, key_f, value_f, probs, rounded, grad_heads):
    prob_grad = jnp.einsum("mhqd,mhkd->mhqk", grad_heads, value_f, precision=lax.Precision.HIGHEST)
    delta = jnp.sum(prob_grad * probs, axis=-1, keepdims=True)
    score_grad = probs * (prob_grad - delta)
    query_gradient = jnp.einsum(
        "mhqk,mhkd->mhqd", score_grad, key_f, precision=lax.Precision.HIGHEST
    ) / math.sqrt(HEAD_SIZE)
    key_term = jnp.einsum(
        "mhqk,mhqd->mhkd", score_grad, query_f, precision=lax.Precision.HIGHEST
    ) / math.sqrt(HEAD_SIZE)
    value_term = jnp.einsum("mhqk,mhqd->mhkd", rounded, grad_heads, precision=lax.Precision.HIGHEST)
    return (query_gradient, key_term, value_term)


def per_device(
    queries,
    slot_keys_values,
    segment_ids,
    residual_in,
    cotangent,
    out_weight,
    live_mask,
    micro_counts,
):
    tensor_size = lax.axis_size("tensor")
    heads_here = QUERY_HEADS // tensor_size
    heads_per_group = QUERY_HEADS // KEY_VALUE_HEADS
    tensor_idx = lax.axis_index("tensor")
    replica_idx = lax.axis_index("dp")
    query_here = queries[0]
    slot_total_count = query_here.shape[0]
    sequence_length = query_here.shape[1]
    local_feats = residual_in.shape[3]
    key_value_local = slot_keys_values[0].reshape(
        slot_total_count, 2, sequence_length, KEY_VALUE_HEADS, HEAD_SIZE
    )
    segments = segment_ids[0]
    head_ids = tensor_idx * heads_here + jnp.arange(heads_here)
    key_value_head_rows = head_ids // heads_per_group
    query_heads = query_here.reshape(
        slot_total_count, sequence_length, heads_here, HEAD_SIZE
    ).transpose(0, 2, 1, 3)
    key_head_rows = jnp.take(key_value_local[:, 0], key_value_head_rows, axis=2).transpose(
        0, 2, 1, 3
    )
    value_heads = jnp.take(key_value_local[:, 1], key_value_head_rows, axis=2).transpose(0, 2, 1, 3)
    positions = jnp.arange(sequence_length)
    allowed = (positions[None, :] <= positions[:, None])[None] & (
        segments[:, :, None] == segments[:, None, :]
    )
    allowed = allowed[:, None]
    scores = jnp.einsum(
        "mhqd,mhkd->mhqk", query_heads, key_head_rows, preferred_element_type=jnp.float32
    ) / math.sqrt(HEAD_SIZE)
    masked = jnp.where(allowed, scores, -jnp.inf)
    top_score = jnp.max(masked, axis=-1, keepdims=True)
    expo = jnp.where(allowed, jnp.exp(masked - top_score), 0.0)
    probs = expo / jnp.sum(expo, axis=-1, keepdims=True)
    probs_low = probs.astype(jnp.bfloat16)
    context = jnp.einsum(
        "mhqk,mhkd->mqhd", probs_low, value_heads, preferred_element_type=jnp.float32
    )
    context = context.astype(jnp.bfloat16).reshape(
        slot_total_count, sequence_length, heads_here * HEAD_SIZE
    )
    context_rows = context.reshape(slot_total_count * sequence_length, heads_here * HEAD_SIZE)
    weight_rows = lax.all_gather(out_weight, "dp", axis=1, tiled=True)
    reduced_total = lax.psum_scatter(
        jnp.einsum(
            "hd,nh->dn", weight_rows, context_rows, preferred_element_type=jnp.float32
        ).astype(jnp.bfloat16),
        "tensor",
        scatter_dimension=0,
        tiled=True,
    ).astype(jnp.float32)
    reduced_total = reduced_total.transpose(1, 0).reshape(
        slot_total_count, sequence_length, local_feats
    )
    block_residual = (residual_in[0].astype(jnp.float32) + reduced_total).astype(jnp.bfloat16)[None]
    replica_pick = jnp.arange(live_mask.shape[0]) == replica_idx
    my_live = jnp.sum(jnp.where(replica_pick, live_mask, 0))
    my_count = jnp.sum(jnp.where(replica_pick, micro_counts, 0))
    live_total = jnp.maximum(jnp.sum(live_mask * micro_counts), 1)
    slot_live = (jnp.arange(slot_total_count) < my_count) & (my_live > 0)
    slot_weight = slot_live.astype(jnp.float32) / live_total.astype(jnp.float32)
    scaled_cot = (cotangent[0].astype(jnp.float32) * slot_weight[:, None, None]).astype(
        jnp.bfloat16
    )
    weight_back = lax.all_gather(out_weight, "dp", axis=1, tiled=True)
    shard_piece = lax.all_gather(scaled_cot, "tensor", axis=2, tiled=True)
    grad_piece = jnp.einsum("msh,msd->hd", context, shard_piece, preferred_element_type=jnp.float32)
    grad_rows = grad_piece
    context_grad = jnp.einsum(
        "msd,hd->msh", shard_piece, weight_back, preferred_element_type=jnp.float32
    )
    grad_rows, context_grad = (grad_rows, context_grad)
    projection_weight_gradient = lax.psum_scatter(
        grad_rows.astype(jnp.bfloat16), "dp", scatter_dimension=1, tiled=True
    ).astype(jnp.float32)
    grad_heads = context_grad.reshape(
        slot_total_count, sequence_length, heads_here, HEAD_SIZE
    ).transpose(0, 2, 1, 3)
    query_f = query_heads.astype(jnp.float32)
    key_f = key_head_rows.astype(jnp.float32)
    value_f = value_heads.astype(jnp.float32)
    rounded = probs_low.astype(jnp.float32)
    query_gradient, key_term, value_term = attention_backward(
        query_f, key_f, value_f, probs, rounded, grad_heads
    )
    query_out = (
        query_gradient.transpose(0, 2, 1, 3)
        .reshape(slot_total_count, sequence_length, heads_here * HEAD_SIZE)
        .astype(jnp.bfloat16)[None]
    )
    addend_terms = (
        jnp.stack([key_term, value_term], axis=1).astype(jnp.bfloat16).astype(jnp.float32)
    )
    head_choice = (key_value_head_rows[:, None] == jnp.arange(KEY_VALUE_HEADS)[None, :]).astype(
        jnp.float32
    )
    positioned = jnp.einsum(
        "mchsd,hk->mcskd", addend_terms, head_choice, precision=lax.Precision.HIGHEST
    )
    positioned = positioned.reshape(
        slot_total_count, 2, sequence_length, KEY_VALUE_HEADS * HEAD_SIZE
    )
    keyval_sum = lax.psum(positioned.astype(jnp.bfloat16), "tensor")
    key_value_gradient = keyval_sum[None]
    return (block_residual, query_out, key_value_gradient, projection_weight_gradient)


def solution(mesh):
    placed = (
        P("dp", None, None, "tensor"),
        P("dp", None, None, None, None),
        P("dp", None, None),
        P("dp", None, None, "tensor"),
        P("dp", None, None, "tensor"),
        P("tensor", "dp"),
        P(),
        P(),
    )
    return jax.shard_map(
        per_device,
        mesh=mesh,
        in_specs=placed,
        out_specs=(
            P("dp", None, None, "tensor"),
            P("dp", None, None, "tensor"),
            P("dp", None, None, None, None),
            P("tensor", "dp"),
        ),
        check_vma=False,
    )
```

profile of v0, /device:TPU:1, one launch (start us, length us, event | category | flops | bytes accessed | tf_op | source)
XLA Modules:
  0.0 764.3 jit_solution(7365205446137784672)
XLA Ops:
  7.2 0.7 all-gather.3.cloned.1.call-update
  8.0 1.3 fusion.41
  10.0 1.1 copy.50
  11.7 0.7 and_select_fusion
  12.4 0.8 fusion.19
  13.2 0.9 reshape_squeeze.7
  14.2 1.5 copy.69
  15.9 0.3 copy_bitcast_fusion
  16.1 0.6 gather_fusion.1
  16.7 0.6 gather_fusion
  17.8 0.2 fusion.45
  18.0 0.3 convolution_convert_fusion.3
  18.4 81.9 %all-gather.3.cloned.1.call-done = bf16[256,4224]{0,1:T(8,128)(2,1)} async-done(((bf16[256,176]{0,1:T(8,128)(2,1)}), bf16[256,4224]{0,1:T(8,128)(2,1)}) %all-gather.3.cloned.1.call-update) | async-done | bytes 2162704 | tf_op jit(solution)/shard_map/all_gather | solution.py:79
  100.3 3.7 fusion.2
  104.1 143.6 %all-gather.5.cloned.1.call-done = bf16[4,64,4224]{1,0,2:T(4,128)(2,1)} async-done(((bf16[4,64,132]{1,0,2:T(4,128)(2,1)}), bf16[4,64,4224]{1,0,2:T(4,128)(2,1)}) %all-gather.5.cloned.1.call-update) | async-done | bytes 2162704 | tf_op jit(solution)/shard_map/all_gather | solution.py:102
  247.6 6.6 copy.51
  254.2 2.4 fusion.11
  256.6 0.3 fusion.16
  256.9 0.4 multiply_reduce_fusion
  257.5 0.3 fusion.17
  258.0 0.6 fusion.5
  258.5 1.3 broadcast_in_dim.51
  259.9 2.3 fusion.1
  262.2 1.3 dynamic-slice
  264.3 0.4 fusion.18
  264.8 0.7 convert_element_type.89
  265.6 331.3 %all-reduce.4.cloned.1.call-done = (bf16[4224,256]{0,1:T(8,128)(2,1)}, bf16[1,4,2,64,1024]{4,3,2,1,0:T(8,128)(2,1)}) async-done(((bf16[4224,256]{0,1:T(8,128)(2,1)}, bf16[1,4,2,64,1024]{4,3,2,1,0:T(8,128)(2,1)}), (bf16[4224,256]{0,1:T(8,128)(2,1)}, bf16[1,4,2,64,1024]{4,3,2,1,0:T(8,128)(2,1)})) %all-reduce.4.cloned.1.call-update) | async-done | bytes 3211280
  596.9 1.0 dynamic-slice_convert_fusion
  597.9 0.7 add_convert_fusion
  598.6 155.3 %reduce-scatter.3.cloned.1.call-done = bf16[256,176]{0,1:T(8,128)(2,1)} async-done(((bf16[256,4224]{0,1:T(8,128)(2,1)}), bf16[256,176]{0,1:T(8,128)(2,1)}) %reduce-scatter.3.cloned.1.call-update) | async-done | bytes 90128 | tf_op jit(solution)/shard_map/reduce_scatter | solution.py:109
  753.9 1.6 convert_element_type.94
  755.5 2.3 copy.113
  (34 shorter events, 1.4 us)
Async XLA Ops:
  7.2 93.2 %all-gather.3.cloned.1.call-start = ((), (), s32[]{:S(2)}) async-start(), calls=%async_computation.1 | async-start | bytes 2252800 | tf_op jit(solution)/shard_map/all_gather | solution.py:79
  7.9 239.7 %all-gather.5.cloned.1.call-start = ((), (), s32[]{:S(2)}) async-start(), calls=%async_computation.2 | async-start | bytes 4460544 | tf_op jit(solution)/shard_map/all_gather | solution.py:102
  13.2 583.7 %all-reduce.4.cloned.1.call-start = ((), (), s32[]{:S(2)}) async-start(), calls=%async_computation.4 | async-start | bytes 6422528
  14.2 3.4 copy-start.2
  15.8 1.6 copy-start.5
  18.0 239.2 %copy-start = (f32[4,2,64,64]{2,3,1,0:T(8,128)}, f32[4,2,64,64]{2,3,1,0:T(8,128)S(1)}, u32[]{:S(2)}) copy-start(f32[4,2,64,64]{2,3,1,0:T(8,128)S(1)} %get-tuple-element.15) | copy-start | bytes 393220
  256.6 0.9 copy-start.3
  257.3 0.7 copy-start.6
  259.8 494.1 %reduce-scatter.3.cloned.1.call-start = ((), (), s32[]{:S(2)}) async-start(), calls=%async_computation.3 | async-start | bytes 2252800 | tf_op jit(solution)/shard_map/reduce_scatter | solution.py:109
  262.2 2.0 copy-start.1
  262.2 2.0 copy-start.7
  262.2 335.7 %copy-start.4 = (bf16[1,4,64,132]{3,2,1,0:T(8,128)(2,1)S(1)}, bf16[1,4,64,132]{3,2,1,0:T(8,128)(2,1)}, u32[]{:S(2)}) copy-start(bf16[1,4,64,132]{3,2,1,0:T(8,128)(2,1)} %param.13) | copy-start | bytes 202756
Sparse Core Ops, SparseCore 0:
  12.0 88.2 all-gather.2
  103.3 144.3 all-gather.4
  260.0 336.8 all-reduce.3
  602.4 151.5 reduce-scatter.2
where the time goes:
time: 765 us; the launch traced here: 764 us
  waiting for transfers between devices  713 us (93%)
  local copies, waits for them, and re-layouts  17.9 us (2%)
  between operations  16.1 us (2%)
  matrix products  10.8 us (1%)
    unnamed x5, waiting for transfers between devices  332 us
    reduce_scatter x1, waiting for transfers between devices, per_device(): lax.psum_scatter(grad_rows.astype(jnp.bfloat16), 'dp', scatter_dimension=...  155 us
    all_gather x1, waiting for transfers between devices, per_device(): shard_piece = lax.all_gather(scaled_cot, 'tensor', axis=2, tiled=True)  144 us
    all_gather x1, waiting for transfers between devices, per_device(): weight_rows = lax.all_gather(out_weight, 'dp', axis=1, tiled=True)  81.9 us
  transfers between devices with their start and end apart: 4, of which 4 were waited for; matrix products, arithmetic and copies ran while one was open for 3% of the time, Pallas kernels for 0%

commit v1 on v0

v1 whole, which is shorter than its diff:
```python
import math

import jax
import jax.numpy as jnp
from jax import lax
from jax.experimental import pallas as pl
from jax.experimental.pallas import tpu as pltpu
from jax.sharding import PartitionSpec as P

HEAD_SIZE = 128
MESH = pl.DeviceIdType.MESH
F32 = jnp.float32
BF16 = jnp.bfloat16

BLOCKS = 96
REAL = 44
ROWS = 48
C_BLOCKS = 3
W_BLOCKS = 4
TOKENS = 256
N_SEND = 176


def dot(a, b, ca, cb):
    return lax.dot_general(a, b, (((ca,), (cb,)), ((), ())), preferred_element_type=F32)


def kernel(
    c_own, w_own, q_ref, kv_hbm, seg_col, seg_row,
    o_res, o_q, o_kv, o_w,
    cg, wg, po, rp, rm, fz, cz, e_send, e_core, es, ex0, ex1, ex2, fe, ez,
    d_own, dz, kvs, ctx, probs, dctx,
    ssem, bsem, asem, rpsem, rmsem, czsem, ecsem, exsem, ezsem, dzsem, kvsem, ldsem,
):
    dpi = lax.axis_index("dp")
    ti = lax.axis_index("tensor")
    core = lax.rem(dpi, 2)
    zh = lax.rem(lax.div(dpi, 2), 3)
    x = lax.div(dpi, 6)
    zl = lax.rem(ti, 4)
    y = lax.div(ti, 4)
    way = 1 - 2 * core

    def y_at(k):
        return lax.rem(y + (k + 8), 8)

    def x_at(k):
        return lax.rem(x + k + 4, 4)

    zlj = [zl, zl + 1 - 2 * lax.rem(zl, 2), lax.rem(zl + 2, 4), 3 - zl]
    zhk = [zh, lax.rem(zh + 1, 3), lax.rem(zh + 2, 3)]
    on_y = {k: (dpi, y_at(k) * 4 + zl) for k in (1, -1)}
    on_zl = [None] + [(dpi, y * 4 + zlj[j]) for j in (1, 2, 3)]
    on_zh = [None] + [((x * 3 + zhk[k]) * 2 + core, ti) for k in (1, 2)]
    on_x = {k: ((x_at(k * way) * 3 + zh) * 2 + core, ti) for k in (1, -1)}
    other = (dpi + way, ti)

    sends = []

    def send(src, dst, sem, device):
        copy = pltpu.make_async_remote_copy(
            src_ref=src, dst_ref=dst, send_sem=ssem.at[len(sends)], recv_sem=sem,
            device_id=device, device_id_type=MESH,
        )
        copy.start()
        sends.append(copy)

    def arrive(dst, sem):
        pltpu.make_async_remote_copy(
            src_ref=dst, dst_ref=dst, send_sem=ssem.at[0], recv_sem=sem,
            device_id=other, device_id_type=MESH,
        ).wait_recv()

    partners = [on_y[1], on_y[-1], *on_zl[1:], *on_zh[1:], on_x[1], on_x[-1], other]
    barrier = pltpu.get_barrier_semaphore()
    for partner in partners:
        pl.semaphore_signal(barrier, inc=1, device_id=partner, device_id_type=MESH)

    load = pltpu.make_async_copy(
        kv_hbm.at[:, :, :, pl.ds(pl.multiple_of(y * HEAD_SIZE, HEAD_SIZE), HEAD_SIZE)], kvs, ldsem
    )
    load.start()

    def c_at(buf, t):
        return buf.at[pl.ds(t * C_BLOCKS, C_BLOCKS)]

    def w_at(buf, d):
        return buf.at[pl.ds(d * W_BLOCKS, W_BLOCKS)]

    cg[pl.ds(ti * C_BLOCKS, C_BLOCKS)] = c_own[...]
    wg[pl.ds(dpi * W_BLOCKS, W_BLOCKS)] = w_own[...]
    load.wait()

    scale = 1.0 / math.sqrt(HEAD_SIZE)

    def attend(head):
        cols = slice(head * HEAD_SIZE, (head + 1) * HEAD_SIZE)
        key = kvs[:, 0].reshape(TOKENS, HEAD_SIZE)
        value = kvs[:, 1].reshape(TOKENS, HEAD_SIZE)
        scores = dot(q_ref[:, cols], key, 1, 1) * scale
        row = lax.broadcasted_iota(jnp.int32, (TOKENS, TOKENS), 0)
        col = lax.broadcasted_iota(jnp.int32, (TOKENS, TOKENS), 1)
        allowed = (col <= row) & (seg_col[...] == seg_row[...])
        scores = jnp.where(allowed, scores, -1e30)
        top = jnp.max(scores, axis=1, keepdims=True)
        expo = jnp.where(allowed, jnp.exp(scores - top), 0.0)
        p = expo / jnp.sum(expo, axis=1, keepdims=True)
        probs[head] = p
        ctx[:, cols] = dot(p.astype(BF16), value, 1, 0).astype(BF16)

    attend(0)
    pl.semaphore_wait(barrier, len(partners))

    def gather_sends(own, place, sem):
        for k in (1, -1):
            send(own, place(ti), sem.at[ti], on_y[k])
        for j in (1, 2, 3):
            send(own, place(ti), sem.at[ti], on_zl[j])

    def gather_step(place, sem, s, j):
        if s == 0:
            t = y * 4 + zlj[j]
            arrive(place(t), sem.at[t])
            for k in (1, -1):
                send(place(t), place(t), sem.at[t], on_y[k])
            return
        for k, mine in ((1, j < 2), (-1, j >= 2)):
            if s == 4 and not mine:
                continue
            t = y_at(-k * s) * 4 + zlj[j]
            arrive(place(t), sem.at[t])
            if s < 3 or (s == 3 and mine):
                send(place(t), place(t), sem.at[t], on_y[k])

    steps = {n: [] for n in range(1, 8)}
    for s in (4, 3, 2, 1, 0):
        for j in range(4):
            if s + j > 0:
                steps[s + j].append((s, j))

    def c_place(t):
        return c_at(cg, t)

    def w_x(k, d_x, zhx, forward):
        d = (d_x * 3 + zhx) * 2 + core
        arrive(w_at(wg, d), asem.at[d])
        if forward:
            send(w_at(wg, d), w_at(wg, d), asem.at[d], on_x[k])
        send(w_at(wg, d), w_at(wg, d), asem.at[d], other)

    def w_x_all(zhx):
        w_x(1, x_at(-way), zhx, True)
        w_x(1, x_at(way), zhx, False)
        w_x(1, x_at(2), zhx, False)

    gather_sends(c_own, c_place, bsem)
    for k in (1, -1):
        send(w_own, w_at(wg, dpi), asem.at[dpi], on_x[k])
    send(w_own, w_at(wg, dpi), asem.at[dpi], other)

    def run_steps(n):
        for s, j in steps[n]:
            gather_step(c_place, bsem, s, j)

    run_steps(1)
    for k in (1, 2):
        send(w_own, w_at(wg, dpi), asem.at[dpi], on_zh[k])
    attend(1)
    run_steps(2)
    w_x_all(zh)
    run_steps(3)
    run_steps(4)
    for k in (1, 2):
        d = (x * 3 + zhk[k]) * 2 + core
        arrive(w_at(wg, d), asem.at[d])
        for m in (1, -1):
            send(w_at(wg, d), w_at(wg, d), asem.at[d], on_x[m])
        send(w_at(wg, d), w_at(wg, d), asem.at[d], other)
    run_steps(5)
    w_x_all(zhk[1])
    run_steps(6)
    w_x_all(zhk[2])
    for xd in range(4):
        for zd in range(3):
            d = (xd * 3 + zd) * 2 + 1 - core
            arrive(w_at(wg, d), asem.at[d])

    def project(i, carry):
        n = 8
        out = dot(wg[pl.ds(i * n, n)].reshape(n * ROWS, TOKENS), ctx[...], 1, 1)
        po[pl.ds(i * n, n)] = out.astype(BF16).reshape(n, ROWS, TOKENS)
        return carry

    lax.fori_loop(0, BLOCKS // 8, project, 0)

    recv_buf = {1: (rp, rpsem), -1: (rm, rmsem)}

    def p_at(k, j):
        return c_at(po, y_at(k) * 4 + zlj[j])

    def slot(k, r, j):
        buf, sem = recv_buf[k]
        i = (r - 1) * 4 + j
        return buf.at[i], sem.at[i]

    def starts(k, j):
        return (j < 2) if k == 1 else (j >= 2)

    def ring_first():
        for j in range(4):
            for k in (1, -1):
                if starts(k, j):
                    send(p_at(4, j), *slot(k, 1, j), on_y[k])
        for j in range(4):
            for k in (1, -1):
                if not starts(k, j):
                    send(p_at(3 * k, j), *slot(k, 2, j), on_y[k])

    def ring_step(r):
        for j in range(4):
            for k in (1, -1):
                if r == 1 and not starts(k, j):
                    continue
                buf, sem = slot(k, r, j)
                arrive(buf, sem)
                own = po[pl.ds((y_at(k * (4 - r)) * 4 + zlj[j]) * C_BLOCKS, C_BLOCKS)]
                buf[...] = (buf[...].astype(F32) + own.astype(F32)).astype(BF16)
                send(buf, *slot(k, r + 1, j), on_y[k])

    ring_first()
    run_steps(7)

    def grad_chunk(d):
        return dot(cg[pl.ds(d * W_BLOCKS, W_BLOCKS)].reshape(W_BLOCKS * ROWS, TOKENS), ctx[...], 1, 0)

    for xd in (x_at(2), x_at(way), x_at(-way), x):
        for zd in range(3):
            c12 = xd * 3 + zd
            part = grad_chunk(c12 * 2 + 1 - core).astype(BF16)
            e_send[c12] = part.reshape(W_BLOCKS, ROWS, TOKENS)
            send(e_send.at[c12], e_core.at[c12], ecsem.at[c12], other)

    ring_step(1)

    dctx[...] = jnp.zeros_like(dctx)

    def back(i, carry):
        n = 16
        dctx[...] += dot(
            cg[pl.ds(i * n, n)].reshape(n * ROWS, TOKENS),
            wg[pl.ds(i * n, n)].reshape(n * ROWS, TOKENS), 0, 0,
        )
        return carry

    lax.fori_loop(0, BLOCKS // 16, back, 0)
    ring_step(2)

    def attend_back(head):
        cols = slice(head * HEAD_SIZE, (head + 1) * HEAD_SIZE)
        key = kvs[:, 0].reshape(TOKENS, HEAD_SIZE)
        value = kvs[:, 1].reshape(TOKENS, HEAD_SIZE)
        grad = dctx[:, cols].astype(BF16)
        p = probs[head]
        prob_grad = dot(grad, value, 1, 1)
        delta = jnp.sum(prob_grad * p, axis=1, keepdims=True)
        score_grad = (p * (prob_grad - delta)).astype(BF16)
        o_q[:, cols] = (dot(score_grad, key, 1, 0) * scale).astype(BF16)
        return dot(score_grad, q_ref[:, cols], 0, 0) * scale, dot(p.astype(BF16), grad, 0, 0)

    key_a, value_a = attend_back(0)
    key_b, value_b = attend_back(1)
    d_own[:, 0] = (key_a + key_b).astype(BF16).reshape(4, 64, HEAD_SIZE)
    d_own[:, 1] = (value_a + value_b).astype(BF16).reshape(4, 64, HEAD_SIZE)
    for j in (1, 2, 3):
        send(d_own.at[zlj[j]], dz.at[j], dzsem.at[j], on_zl[j])

    def grad_sum(xd):
        for zd in range(3):
            c12 = xd * 3 + zd
            part = grad_chunk(c12 * 2 + core)
            arrive(e_core.at[c12], ecsem.at[c12])
            part = part.reshape(W_BLOCKS, ROWS, TOKENS) + e_core[c12].astype(F32)
            es[c12] = part.astype(BF16)

    grad_sum(x_at(2))
    for zd in range(3):
        send(es.at[x_at(2) * 3 + zd], ex0.at[zd], exsem.at[zd], on_x[1])
    grad_sum(x_at(-way))
    for zd in range(3):
        send(es.at[x_at(-way) * 3 + zd], ex2.at[zd], exsem.at[6 + zd], on_x[-1])
    ring_step(3)

    def kv_place(t):
        lanes = pl.ds(pl.multiple_of(lax.div(t, 4) * HEAD_SIZE, HEAD_SIZE), HEAD_SIZE)
        return o_kv.at[lax.rem(t, 4), :, :, lanes]

    total = d_own[zl].astype(F32)
    for j in (1, 2, 3):
        arrive(dz.at[j], dzsem.at[j])
        total = total + dz[j].astype(F32)
    d_sum = total.astype(BF16)
    dz[0] = d_sum
    o_kv[zl, :, :, pl.ds(pl.multiple_of(y * HEAD_SIZE, HEAD_SIZE), HEAD_SIZE)] = d_sum
    gather_sends(dz.at[0], kv_place, kvsem)

    grad_sum(x_at(way))
    for zd in range(3):
        c12 = x_at(way) * 3 + zd
        arrive(ex0.at[zd], exsem.at[zd])
        ex0[zd] = (ex0[zd].astype(F32) + es[c12].astype(F32)).astype(BF16)
        send(ex0.at[zd], ex1.at[zd], exsem.at[3 + zd], on_x[1])

    mine = None
    for j in (1, 2, 3, 0):
        acc = po[pl.ds((y * 4 + zlj[j]) * C_BLOCKS, C_BLOCKS)].astype(F32)
        for k in (1, -1):
            buf, sem = slot(k, 4, j)
            arrive(buf, sem)
            acc = acc + buf[...].astype(F32)
        if j:
            fz[j] = acc.astype(BF16)
            send(fz.at[j], cz.at[j], czsem.at[j], on_zl[j])
        else:
            o_res[...] = acc

    for n in (1, 2, 3):
        for s, j in steps[n]:
            gather_step(kv_place, kvsem, s, j)

    grad_sum(x)
    for zd in range(3):
        arrive(ex1.at[zd], exsem.at[3 + zd])
        arrive(ex2.at[zd], exsem.at[6 + zd])

    def arrived(zd):
        return es[x * 3 + zd].astype(F32) + ex1[zd].astype(F32) + ex2[zd].astype(F32)

    for k in (1, 2):
        fe[k] = arrived(zhk[k]).astype(BF16)
        send(fe.at[k], ez.at[k], ezsem.at[k], on_zh[k])
    o_w[...] = arrived(zh)

    for n in (4, 5, 6):
        for s, j in steps[n]:
            gather_step(kv_place, kvsem, s, j)
    for j in (1, 2, 3):
        arrive(cz.at[j], czsem.at[j])
        o_res[...] += cz[j].astype(F32)
    for k in (1, 2):
        arrive(ez.at[k], ezsem.at[k])
        o_w[...] += ez[k].astype(F32)
    for s, j in steps[7]:
        gather_step(kv_place, kvsem, s, j)

    for copy in sends:
        copy.wait_send()


def exchange(c_own, w_own, q, kv, seg_col, seg_row):
    c_shape = (C_BLOCKS, ROWS, TOKENS)
    w_shape = (W_BLOCKS, ROWS, TOKENS)
    vmem = pl.BlockSpec(memory_space=pltpu.VMEM)
    dma = pltpu.SemaphoreType.DMA
    return pl.pallas_call(
        kernel,
        out_shape=(
            jax.ShapeDtypeStruct(c_shape, F32),
            jax.ShapeDtypeStruct((TOKENS, TOKENS), BF16),
            jax.ShapeDtypeStruct(kv.shape, BF16),
            jax.ShapeDtypeStruct(w_shape, F32),
        ),
        in_specs=[vmem, vmem, vmem, pl.BlockSpec(memory_space=pl.ANY), vmem, vmem],
        out_specs=(vmem, vmem, vmem, vmem),
        scratch_shapes=[
            pltpu.VMEM((BLOCKS, ROWS, TOKENS), BF16),
            pltpu.VMEM((BLOCKS, ROWS, TOKENS), BF16),
            pltpu.VMEM((BLOCKS, ROWS, TOKENS), BF16),
            pltpu.VMEM((16, *c_shape), BF16),
            pltpu.VMEM((16, *c_shape), BF16),
            pltpu.VMEM((4, *c_shape), BF16),
            pltpu.VMEM((4, *c_shape), BF16),
            pltpu.VMEM((12, *w_shape), BF16),
            pltpu.VMEM((12, *w_shape), BF16),
            pltpu.VMEM((12, *w_shape), BF16),
            pltpu.VMEM((3, *w_shape), BF16),
            pltpu.VMEM((3, *w_shape), BF16),
            pltpu.VMEM((3, *w_shape), BF16),
            pltpu.VMEM((3, *w_shape), BF16),
            pltpu.VMEM((3, *w_shape), BF16),
            pltpu.VMEM((4, 2, 64, HEAD_SIZE), BF16),
            pltpu.VMEM((4, 2, 64, HEAD_SIZE), BF16),
            pltpu.VMEM((4, 2, 64, HEAD_SIZE), BF16),
            pltpu.VMEM((TOKENS, TOKENS), BF16),
            pltpu.VMEM((2, TOKENS, TOKENS), F32),
            pltpu.VMEM((TOKENS, TOKENS), F32),
            dma((N_SEND,)),
            dma((32,)),
            dma((24,)),
            dma((16,)),
            dma((16,)),
            dma((4,)),
            dma((12,)),
            dma((9,)),
            dma((3,)),
            dma((4,)),
            dma((32,)),
            dma(()),
        ],
        compiler_params=pltpu.CompilerParams(
            collective_id=0, has_side_effects=True, vmem_limit_bytes=48 * 1024 * 1024
        ),
    )(c_own, w_own, q, kv, seg_col, seg_row)


def padded(rows, blocks):
    return jnp.pad(rows.reshape(blocks, REAL, TOKENS), ((0, 0), (0, ROWS - REAL), (0, 0)))


def per_device(
    queries, slot_keys_values, segment_ids, residual_in, cotangent, out_weight, live_mask, micro_counts
):
    replica = lax.axis_index("dp")
    slots = queries.shape[1]
    pick = jnp.arange(live_mask.shape[0]) == replica
    my_live = jnp.sum(jnp.where(pick, live_mask, 0))
    my_count = jnp.sum(jnp.where(pick, micro_counts, 0))
    live_total = jnp.maximum(jnp.sum(live_mask * micro_counts), 1)
    slot_live = (jnp.arange(slots) < my_count) & (my_live > 0)
    slot_weight = slot_live.astype(F32) / live_total.astype(F32)
    scaled = (cotangent[0].astype(F32) * slot_weight[:, None, None]).astype(BF16)
    c_own = padded(scaled.reshape(TOKENS, -1).T, C_BLOCKS)
    w_own = padded(out_weight.T, W_BLOCKS)
    seg = (segment_ids[0] + 8 * jnp.arange(slots)[:, None]).reshape(TOKENS)
    res, q_grad, kv_grad, w_grad = exchange(
        c_own, w_own, queries[0].reshape(TOKENS, TOKENS), slot_keys_values[0],
        seg.reshape(TOKENS, 1), seg.reshape(1, TOKENS),
    )
    total = res[:, :REAL].reshape(C_BLOCKS * REAL, TOKENS).T.reshape(residual_in.shape)
    block_residual = (residual_in.astype(F32) + total).astype(BF16)
    w_grad = w_grad[:, :REAL].reshape(W_BLOCKS * REAL, TOKENS).T
    return (block_residual, q_grad.reshape(queries.shape), kv_grad[None], w_grad)


def solution(mesh):
    placed = (
        P("dp", None, None, "tensor"),
        P("dp", None, None, None, None),
        P("dp", None, None),
        P("dp", None, None, "tensor"),
        P("dp", None, None, "tensor"),
        P("tensor", "dp"),
        P(),
        P(),
    )
    return jax.shard_map(
        per_device,
        mesh=mesh,
        in_specs=placed,
        out_specs=(
            P("dp", None, None, "tensor"),
            P("dp", None, None, "tensor"),
            P("dp", None, None, None, None),
            P("tensor", "dp"),
        ),
        check_vma=False,
    )
```

time: 765 us -> 118 us (0.15)
  the two profiles are of different devices: /device:TPU:1 before, /device:TPU:8 now
where the time goes in v1:
time: 118 us
  Pallas kernels  105 us (89%)
  local copies, waits for them, and re-layouts  7.24 us (6%)
  other arithmetic  3.63 us (3%)
  between operations  2.11 us (2%)
    pallas_call x1, Pallas kernels, exchange(): pl.pallas_call(kernel, out_shape=(jax.ShapeDtypeStruct(c_shape, F32), jax...  105 us
    unnamed x8, local copies, waits for them, and re-layouts  3.24 us

profile of v1, /device:TPU:8, one launch (start us, length us, event | category | flops | bytes accessed | tf_op | source)
XLA Modules:
  0.0 117.9 jit_solution(8019452051914472679)
XLA Ops:
  0.6 0.0 copy-start
  0.7 0.8 squeeze.11
  1.5 0.8 squeeze.10
  2.3 1.3 %fusion.1 = (s32[]{:T(128)}, s32[]{:T(128)}, s32[]{:T(128)}) fusion(s32[24]{0:T(128)} %param.15, s32[]{:T(128)S(6)} %axis_index.15, s32[24]{0:T(128)} %param.14), kind=kLoop, calls=%fused_computation.7 | loop fusion | flops 165 | bytes 208 | tf_op jit(solution)/shard_map/reduce_sum | solution.py:426
  5.0 0.7 and_select_fusion
  5.6 0.1 add.37
  5.7 0.1 add.40
  5.8 0.1 add.38
  5.9 0.1 mul.27
  5.9 0.1 mul.28
  6.0 0.9 reshape.81
  6.9 0.1 copy.19.seg_col
  7.1 0.9 bitcast_convert_fusion
  8.0 0.1 copy.18
  8.1 0.0 copy-start.1
  8.2 0.0 copy-done
  8.2 0.8 copy-done.1
  9.1 104.9 %shard_map.111 = (f32[3,48,256]{2,1,0:T(8,128)S(1)}, bf16[256,256]{1,0:T(8,128)(2,1)S(1)}, bf16[4,2,64,1024]{3,2,1,0:T(8,128)(2,1)S(1)}, f32[4,48,256]{2,1,0:T(8,128)S(1)}) custom-call(bf16[3,48,256]{2,1,0:T(8,128)(2,1)S(1)} %pad.8.c_own, bf16[4,48,256]{2,1,0:T(8,128)(2,1)S(1)} %pad.9.w_own, bf16[256,256]{1,0:T(8,128)(2,1)S(1)} %bitcast.19, ...), custom_call_target="tpu_custom_call" | custom-call | tf_op jit(solution)/shard_map/pallas_call | solution.py:364
  114.0 0.0 copy-start.2
  114.0 0.1 copy.20
  114.1 0.8 copy-done.2
  114.9 0.7 add_convert_fusion
  115.6 0.7 reshape.85
  116.3 0.7 copy.23
  116.9 1.0 copy.24
  (8 shorter events, 0.1 us)
Async XLA Ops:
  0.6 7.6 %copy-start = (bf16[1,4,2,64,1024]{4,3,2,1,0:T(8,128)(2,1)S(1)}, bf16[1,4,2,64,1024]{4,3,2,1,0:T(8,128)(2,1)}, u32[]{:S(2)}) copy-start(bf16[1,4,2,64,1024]{4,3,2,1,0:T(8,128)(2,1)} %param.9) | copy-start | bytes 3145732
  8.1 0.9 copy-start.1
  114.0 0.9 copy-start.2

commit v2 on v1

v2 whole, which is shorter than its diff:
```python
import math

import jax
import jax.numpy as jnp
from jax import lax
from jax.experimental import pallas as pl
from jax.experimental.pallas import tpu as pltpu
from jax.sharding import PartitionSpec as P

HEAD_SIZE = 128
MESH = pl.DeviceIdType.MESH
F32 = jnp.float32
BF16 = jnp.bfloat16

BLOCKS = 96
REAL = 44
ROWS = 48
C_BLOCKS = 3
W_BLOCKS = 4
TOKENS = 256
N_SEND = 176


def dot(a, b, ca, cb):
    return lax.dot_general(a, b, (((ca,), (cb,)), ((), ())), preferred_element_type=F32)


def one_hot(rows, cols):
    row = lax.broadcasted_iota(jnp.int32, (rows, cols), 0)
    col = lax.broadcasted_iota(jnp.int32, (rows, cols), 1)
    offset = lax.rem(row, ROWS)
    return jnp.where((col == lax.div(row, ROWS) * REAL + offset) & (offset < REAL), 1.0, 0.0).astype(BF16)


def kernel(
    cot_ref, w_ref, q_ref, kv_hbm, seg_ref, res_ref, live_ref, count_ref,
    o_res, o_q, o_kv, o_w,
    c_own, w_own, cg, wg, po, rp, rm, fz, cz, e_send, e_core, es, ex0, ex1, ex2, fe, ez,
    d_own, dz, kvs, ctx, bias, probs, dctx,
    ssem, bsem, asem, rpsem, rmsem, czsem, ecsem, exsem, ezsem, dzsem, kvsem, ldsem,
):
    dpi = lax.axis_index("dp")
    ti = lax.axis_index("tensor")
    core = lax.rem(dpi, 2)
    zh = lax.rem(lax.div(dpi, 2), 3)
    x = lax.div(dpi, 6)
    zl = lax.rem(ti, 4)
    y = lax.div(ti, 4)
    way = 1 - 2 * core

    def y_at(k):
        return lax.rem(y + (k + 8), 8)

    def x_at(k):
        return lax.rem(x + k + 4, 4)

    zlj = [zl, zl + 1 - 2 * lax.rem(zl, 2), lax.rem(zl + 2, 4), 3 - zl]
    zhk = [zh, lax.rem(zh + 1, 3), lax.rem(zh + 2, 3)]
    on_y = {k: (dpi, y_at(k) * 4 + zl) for k in (1, -1)}
    on_zl = [None] + [(dpi, y * 4 + zlj[j]) for j in (1, 2, 3)]
    on_zh = [None] + [((x * 3 + zhk[k]) * 2 + core, ti) for k in (1, 2)]
    on_x = {k: ((x_at(k * way) * 3 + zh) * 2 + core, ti) for k in (1, -1)}
    other = (dpi + way, ti)

    sends = []

    def send(src, dst, sem, device):
        copy = pltpu.make_async_remote_copy(
            src_ref=src, dst_ref=dst, send_sem=ssem.at[len(sends)], recv_sem=sem,
            device_id=device, device_id_type=MESH,
        )
        copy.start()
        sends.append(copy)

    def arrive(dst, sem):
        pltpu.make_async_remote_copy(
            src_ref=dst, dst_ref=dst, send_sem=ssem.at[0], recv_sem=sem,
            device_id=other, device_id_type=MESH,
        ).wait_recv()

    partners = [on_y[1], on_y[-1], *on_zl[1:], *on_zh[1:], on_x[1], on_x[-1], other]
    barrier = pltpu.get_barrier_semaphore()
    for partner in partners:
        pl.semaphore_signal(barrier, inc=1, device_id=partner, device_id_type=MESH)

    load = pltpu.make_async_copy(
        kv_hbm.at[:, :, :, pl.ds(pl.multiple_of(y * HEAD_SIZE, HEAD_SIZE), HEAD_SIZE)], kvs, ldsem
    )
    load.start()

    units = 0
    for r in range(live_ref.shape[0]):
        units = units + live_ref[r] * count_ref[r]
    slot = lax.div(lax.broadcasted_iota(jnp.int32, (TOKENS, 1), 0), 64)
    counted = jnp.where(slot < count_ref[dpi], 1, 0) * jnp.where(live_ref[dpi] > 0, 1, 0)
    weight = counted.astype(F32) / jnp.full((TOKENS, 1), jnp.maximum(units, 1), jnp.int32).astype(F32)
    scaled = (cot_ref[...].astype(F32) * weight).astype(BF16)
    c_hot = one_hot(C_BLOCKS * ROWS, cot_ref.shape[1])
    c_block = dot(c_hot, scaled, 1, 1).astype(BF16).reshape(C_BLOCKS, ROWS, TOKENS)
    c_own[...] = c_block
    cg[pl.ds(ti * C_BLOCKS, C_BLOCKS)] = c_block
    w_block = dot(one_hot(W_BLOCKS * ROWS, w_ref.shape[0]), w_ref[...], 1, 0)
    w_block = w_block.astype(BF16).reshape(W_BLOCKS, ROWS, TOKENS)
    w_own[...] = w_block
    wg[pl.ds(dpi * W_BLOCKS, W_BLOCKS)] = w_block

    def c_place(t):
        return cg.at[pl.ds(t * C_BLOCKS, C_BLOCKS)]

    def w_place(d):
        return wg.at[pl.ds(d * W_BLOCKS, W_BLOCKS)]

    scale = 1.0 / math.sqrt(HEAD_SIZE)

    def mask():
        row = lax.broadcasted_iota(jnp.int32, (TOKENS, TOKENS), 0)
        col = lax.broadcasted_iota(jnp.int32, (TOKENS, TOKENS), 1)
        at = lax.broadcasted_iota(jnp.int32, (64, TOKENS), 0)
        token = lax.broadcasted_iota(jnp.int32, (64, TOKENS), 1)
        tile = jnp.where(lax.rem(token, 64) == at, 1.0, 0.0).astype(BF16)
        seg = seg_ref[...].astype(F32).astype(BF16)
        across = dot(seg, tile, 1, 0)
        down = dot(tile, seg, 0, 1)
        keep = lax.div(lax.broadcasted_iota(jnp.int32, (4, TOKENS), 1), 64)
        keep = keep == lax.broadcasted_iota(jnp.int32, (4, TOKENS), 0)
        seg_row = jnp.sum(jnp.where(keep, across, 0.0), axis=0, keepdims=True)
        keep = lax.div(lax.broadcasted_iota(jnp.int32, (TOKENS, 4), 0), 64)
        keep = keep == lax.broadcasted_iota(jnp.int32, (TOKENS, 4), 1)
        seg_col = jnp.sum(jnp.where(keep, down, 0.0), axis=1, keepdims=True)
        allowed = (col <= row) & (lax.div(col, 64) == lax.div(row, 64)) & (seg_col == seg_row)
        bias[...] = jnp.where(allowed, 0.0, -1e30)

    def attend(head):
        cols = slice(head * HEAD_SIZE, (head + 1) * HEAD_SIZE)
        key = kvs[:, 0].reshape(TOKENS, HEAD_SIZE)
        value = kvs[:, 1].reshape(TOKENS, HEAD_SIZE)
        scores = dot(q_ref[:, cols], key, 1, 1) * scale + bias[...]
        top = jnp.max(scores, axis=1, keepdims=True)
        expo = jnp.exp(scores - top)
        p = expo / jnp.sum(expo, axis=1, keepdims=True)
        probs[head] = p
        ctx[:, cols] = dot(p.astype(BF16), value, 1, 0).astype(BF16)

    def gather_step(place, sem, s, j):
        if s == 0:
            t = y * 4 + zlj[j]
            arrive(place(t), sem.at[t])
            for k in (1, -1):
                send(place(t), place(t), sem.at[t], on_y[k])
            return
        for k, mine in ((1, j < 2), (-1, j >= 2)):
            if s == 4 and not mine:
                continue
            t = y_at(-k * s) * 4 + zlj[j]
            arrive(place(t), sem.at[t])
            if s < 3 or (s == 3 and mine):
                send(place(t), place(t), sem.at[t], on_y[k])

    steps = {n: [] for n in range(1, 11)}
    for s in (4, 3, 2, 1, 0):
        for j in range(4):
            if s + j > 0:
                steps[s + 2 * j].append((s, j))

    def c_steps(*ns):
        for n in ns:
            for s, j in steps[n]:
                gather_step(c_place, bsem, s, j)

    def w_x(d_x, zhx, forward):
        d = (d_x * 3 + zhx) * 2 + core
        arrive(w_place(d), asem.at[d])
        if forward:
            send(w_place(d), w_place(d), asem.at[d], on_x[1])
        send(w_place(d), w_place(d), asem.at[d], other)

    def w_x_all(zhx):
        w_x(x_at(-way), zhx, True)
        w_x(x_at(way), zhx, False)
        w_x(x_at(2), zhx, False)

    def project(i, carry):
        n = 8
        out = dot(wg[pl.ds(i * n, n)].reshape(n * ROWS, TOKENS), ctx[...], 1, 1)
        po[pl.ds(i * n, n)] = out.astype(BF16).reshape(n, ROWS, TOKENS)
        return carry

    recv_buf = {1: (rp, rpsem), -1: (rm, rmsem)}

    def p_at(k, j):
        return po.at[pl.ds((y_at(k) * 4 + zlj[j]) * C_BLOCKS, C_BLOCKS)]

    def ring_slot(k, r, j):
        buf, sem = recv_buf[k]
        i = (r - 1) * 4 + j
        return buf.at[i], sem.at[i]

    def starts(k, j):
        return (j < 2) if k == 1 else (j >= 2)

    def ring_first():
        for j in range(4):
            for k in (1, -1):
                if starts(k, j):
                    send(p_at(4, j), *ring_slot(k, 1, j), on_y[k])
        for j in range(4):
            for k in (1, -1):
                if not starts(k, j):
                    send(p_at(3 * k, j), *ring_slot(k, 2, j), on_y[k])

    def ring_step(r):
        for j in range(4):
            for k in (1, -1):
                if r == 1 and not starts(k, j):
                    continue
                buf, _ = recv_buf[k]
                i = (r - 1) * 4 + j
                arrive(*ring_slot(k, r, j))
                own = po[pl.ds((y_at(k * (4 - r)) * 4 + zlj[j]) * C_BLOCKS, C_BLOCKS)]
                buf[i] = (buf[i].astype(F32) + own.astype(F32)).astype(BF16)
                send(ring_slot(k, r, j)[0], *ring_slot(k, r + 1, j), on_y[k])

    def ring_last(j):
        acc = po[pl.ds((y * 4 + zlj[j]) * C_BLOCKS, C_BLOCKS)].astype(F32)
        for k in (1, -1):
            arrive(*ring_slot(k, 4, j))
            acc = acc + recv_buf[k][0][12 + j].astype(F32)
        return acc

    def grad_chunk(d):
        return dot(cg[pl.ds(d * W_BLOCKS, W_BLOCKS)].reshape(W_BLOCKS * ROWS, TOKENS), ctx[...], 1, 0)

    def grad_share(xd):
        for zd in range(3):
            c12 = xd * 3 + zd
            part = grad_chunk(c12 * 2 + 1 - core).astype(BF16)
            e_send[c12] = part.reshape(W_BLOCKS, ROWS, TOKENS)
            send(e_send.at[c12], e_core.at[c12], ecsem.at[c12], other)

    def grad_sum(xd):
        for zd in range(3):
            c12 = xd * 3 + zd
            part = grad_chunk(c12 * 2 + core)
            arrive(e_core.at[c12], ecsem.at[c12])
            part = part.reshape(W_BLOCKS, ROWS, TOKENS) + e_core[c12].astype(F32)
            es[c12] = part.astype(BF16)

    def back(i, carry):
        n = 16
        dctx[...] += dot(
            cg[pl.ds(i * n, n)].reshape(n * ROWS, TOKENS),
            wg[pl.ds(i * n, n)].reshape(n * ROWS, TOKENS), 0, 0,
        )
        return carry

    def attend_back(head):
        cols = slice(head * HEAD_SIZE, (head + 1) * HEAD_SIZE)
        key = kvs[:, 0].reshape(TOKENS, HEAD_SIZE)
        value = kvs[:, 1].reshape(TOKENS, HEAD_SIZE)
        grad = dctx[:, cols].astype(BF16)
        p = probs[head]
        prob_grad = dot(grad, value, 1, 1)
        delta = jnp.sum(prob_grad * p, axis=1, keepdims=True)
        score_grad = (p * (prob_grad - delta)).astype(BF16)
        o_q[:, cols] = (dot(score_grad, key, 1, 0) * scale).astype(BF16)
        return dot(score_grad, q_ref[:, cols], 0, 0) * scale, dot(p.astype(BF16), grad, 0, 0)

    def kv_place(t):
        lanes = pl.ds(pl.multiple_of(lax.div(t, 4) * HEAD_SIZE, HEAD_SIZE), HEAD_SIZE)
        return o_kv.at[lax.rem(t, 4), :, :, lanes]

    def kv_steps(*pairs):
        for s, j in pairs:
            gather_step(kv_place, kvsem, s, j)

    pl.semaphore_wait(barrier, len(partners))

    for k in (1, -1):
        send(c_own, c_place(ti), bsem.at[ti], on_y[k])
    send(c_own, c_place(ti), bsem.at[ti], on_zl[1])
    for k in (1, 2):
        send(w_own, w_place(dpi), asem.at[dpi], on_zh[k])
    for k in (1, -1):
        send(w_own, w_place(dpi), asem.at[dpi], on_x[k])
    send(w_own, w_place(dpi), asem.at[dpi], other)
    for j in (2, 3):
        send(c_own, c_place(ti), bsem.at[ti], on_zl[j])

    load.wait()
    mask()
    attend(0)
    c_steps(1)
    attend(1)
    c_steps(2)
    w_x_all(zh)
    c_steps(3, 4)
    for k in (1, 2):
        d = (x * 3 + zhk[k]) * 2 + core
        arrive(w_place(d), asem.at[d])
        for m in (1, -1):
            send(w_place(d), w_place(d), asem.at[d], on_x[m])
        send(w_place(d), w_place(d), asem.at[d], other)
    c_steps(5, 6)
    w_x_all(zhk[1])
    c_steps(7, 8)
    w_x_all(zhk[2])
    for xd in range(4):
        for zd in range(3):
            d = (xd * 3 + zd) * 2 + 1 - core
            arrive(w_place(d), asem.at[d])

    lax.fori_loop(0, BLOCKS // 8, project, 0)
    ring_first()
    c_steps(9, 10)

    for xd in (x_at(2), x_at(way), x_at(-way), x):
        grad_share(xd)
    dctx[...] = jnp.zeros_like(dctx)
    lax.fori_loop(0, BLOCKS // 16, back, 0)
    ring_step(1)
    key_a, value_a = attend_back(0)
    key_b, value_b = attend_back(1)
    d_own[:, 0] = (key_a + key_b).astype(BF16).reshape(4, 64, HEAD_SIZE)
    d_own[:, 1] = (value_a + value_b).astype(BF16).reshape(4, 64, HEAD_SIZE)
    for j in (1, 2, 3):
        send(d_own.at[zlj[j]], dz.at[j], dzsem.at[j], on_zl[j])

    grad_sum(x_at(2))
    for zd in range(3):
        send(es.at[x_at(2) * 3 + zd], ex0.at[zd], exsem.at[zd], on_x[1])
    grad_sum(x_at(-way))
    for zd in range(3):
        send(es.at[x_at(-way) * 3 + zd], ex2.at[zd], exsem.at[6 + zd], on_x[-1])
    ring_step(2)

    total = d_own[zl].astype(F32)
    for j in (1, 2, 3):
        arrive(dz.at[j], dzsem.at[j])
        total = total + dz[j].astype(F32)
    d_sum = total.astype(BF16)
    dz[0] = d_sum
    o_kv[zl, :, :, pl.ds(pl.multiple_of(y * HEAD_SIZE, HEAD_SIZE), HEAD_SIZE)] = d_sum
    for k in (1, -1):
        send(dz.at[0], kv_place(ti), kvsem.at[ti], on_y[k])
    for j in (1, 2, 3):
        send(dz.at[0], kv_place(ti), kvsem.at[ti], on_zl[j])

    grad_sum(x_at(way))
    for zd in range(3):
        c12 = x_at(way) * 3 + zd
        arrive(ex0.at[zd], exsem.at[zd])
        ex0[zd] = (ex0[zd].astype(F32) + es[c12].astype(F32)).astype(BF16)
        send(ex0.at[zd], ex1.at[zd], exsem.at[3 + zd], on_x[1])
    grad_sum(x)
    ring_step(3)

    kv_steps((0, 1), (0, 2), (0, 3), (1, 0))

    for zd in range(3):
        arrive(ex1.at[zd], exsem.at[3 + zd])
        arrive(ex2.at[zd], exsem.at[6 + zd])

    def arrived(zd):
        return es[x * 3 + zd].astype(F32) + ex1[zd].astype(F32) + ex2[zd].astype(F32)

    for k in (1, 2):
        fe[k] = arrived(zhk[k]).astype(BF16)
        send(fe.at[k], ez.at[k], ezsem.at[k], on_zh[k])

    for j in (1, 2, 3):
        fz[j] = ring_last(j).astype(BF16)
        send(fz.at[j], cz.at[j], czsem.at[j], on_zl[j])

    kv_steps((1, 1), (2, 0), (1, 2), (2, 1), (1, 3), (3, 0))
    acc = ring_last(0)
    w_sum = arrived(zh)
    kv_steps((2, 2), (3, 1), (2, 3), (3, 2), (3, 3))

    for j in (1, 2, 3):
        arrive(cz.at[j], czsem.at[j])
        acc = acc + cz[j].astype(F32)
    acc = acc.reshape(C_BLOCKS * ROWS, TOKENS)
    left = acc
    out = res_ref[...].astype(F32)
    turned = None
    for _ in range(3):
        part = left.astype(BF16)
        left = left - part.astype(F32)
        piece = dot(part, c_hot, 0, 0)
        turned = piece if turned is None else turned + piece
    o_res[...] = (out + turned).astype(BF16)

    for k in (1, 2):
        arrive(ez.at[k], ezsem.at[k])
        w_sum = w_sum + ez[k].astype(F32)
    for block in range(W_BLOCKS):
        o_w[pl.ds(block * REAL, REAL), :] = w_sum[block, :REAL]

    kv_steps((4, 0), (4, 1), (4, 2), (4, 3))

    for copy in sends:
        copy.wait_send()


def exchange(cot, w, q, kv, seg, res, live, counts):
    c_shape = (C_BLOCKS, ROWS, TOKENS)
    w_shape = (W_BLOCKS, ROWS, TOKENS)
    d_shape = (4, 2, 64, HEAD_SIZE)
    vmem = pl.BlockSpec(memory_space=pltpu.VMEM)
    smem = pl.BlockSpec(memory_space=pltpu.SMEM)
    dma = pltpu.SemaphoreType.DMA
    return pl.pallas_call(
        kernel,
        out_shape=(
            jax.ShapeDtypeStruct(res.shape, BF16),
            jax.ShapeDtypeStruct(q.shape, BF16),
            jax.ShapeDtypeStruct(kv.shape, BF16),
            jax.ShapeDtypeStruct(w.shape, F32),
        ),
        in_specs=[vmem, vmem, vmem, pl.BlockSpec(memory_space=pl.ANY), vmem, vmem, smem, smem],
        out_specs=(vmem, vmem, vmem, vmem),
        scratch_shapes=[
            pltpu.VMEM(c_shape, BF16),
            pltpu.VMEM(w_shape, BF16),
            pltpu.VMEM((BLOCKS, ROWS, TOKENS), BF16),
            pltpu.VMEM((BLOCKS, ROWS, TOKENS), BF16),
            pltpu.VMEM((BLOCKS, ROWS, TOKENS), BF16),
            pltpu.VMEM((16, *c_shape), BF16),
            pltpu.VMEM((16, *c_shape), BF16),
            pltpu.VMEM((4, *c_shape), BF16),
            pltpu.VMEM((4, *c_shape), BF16),
            pltpu.VMEM((12, *w_shape), BF16),
            pltpu.VMEM((12, *w_shape), BF16),
            pltpu.VMEM((12, *w_shape), BF16),
            pltpu.VMEM((3, *w_shape), BF16),
            pltpu.VMEM((3, *w_shape), BF16),
            pltpu.VMEM((3, *w_shape), BF16),
            pltpu.VMEM((3, *w_shape), BF16),
            pltpu.VMEM((3, *w_shape), BF16),
            pltpu.VMEM(d_shape, BF16),
            pltpu.VMEM(d_shape, BF16),
            pltpu.VMEM(d_shape, BF16),
            pltpu.VMEM((TOKENS, TOKENS), BF16),
            pltpu.VMEM((TOKENS, TOKENS), F32),
            pltpu.VMEM((2, TOKENS, TOKENS), F32),
            pltpu.VMEM((TOKENS, TOKENS), F32),
            dma((N_SEND,)),
            dma((32,)),
            dma((24,)),
            dma((16,)),
            dma((16,)),
            dma((4,)),
            dma((12,)),
            dma((9,)),
            dma((3,)),
            dma((4,)),
            dma((32,)),
            dma(()),
        ],
        compiler_params=pltpu.CompilerParams(
            collective_id=0, has_side_effects=True, vmem_limit_bytes=48 * 1024 * 1024
        ),
    )(cot, w, q, kv, seg, res, live, counts)


def per_device(
    queries, slot_keys_values, segment_ids, residual_in, cotangent, out_weight, live_mask, micro_counts
):
    res, q_grad, kv_grad, w_grad = exchange(
        cotangent.reshape(TOKENS, -1), out_weight.T, queries.reshape(TOKENS, TOKENS),
        slot_keys_values[0], segment_ids[0], residual_in.reshape(TOKENS, -1), live_mask, micro_counts,
    )
    return (
        res.reshape(residual_in.shape), q_grad.reshape(queries.shape), kv_grad[None], w_grad.T
    )


def solution(mesh):
    placed = (
        P("dp", None, None, "tensor"),
        P("dp", None, None, None, None),
        P("dp", None, None),
        P("dp", None, None, "tensor"),
        P("dp", None, None, "tensor"),
        P("tensor", "dp"),
        P(),
        P(),
    )
    return jax.shard_map(
        per_device,
        mesh=mesh,
        in_specs=placed,
        out_specs=(
            P("dp", None, None, "tensor"),
            P("dp", None, None, "tensor"),
            P("dp", None, None, None, None),
            P("tensor", "dp"),
        ),
        check_vma=False,
    )
```

time: 118 us -> 125 us (1.059)
  the two profiles are of different devices: /device:TPU:8 before, /device:TPU:2 now
where the time goes in v2:
time: 125 us
  Pallas kernels  116 us (93%)
  local copies, waits for them, and re-layouts  8.44 us (7%)
    pallas_call x1, Pallas kernels, exchange(): pl.pallas_call(kernel, out_shape=(jax.ShapeDtypeStruct(res.shape, BF16),...  116 us
    unnamed x20, local copies, waits for them, and re-layouts  8.44 us

profile of v2, /device:TPU:2, one launch (start us, length us, event | category | flops | bytes accessed | tf_op | source)
XLA Modules:
  0.0 125.0 jit_solution(17182251118304607499)
XLA Ops:
  0.6 0.0 copy-start.5
  0.6 0.0 copy-start.6
  0.7 0.0 copy-start.7
  0.7 0.7 copy-done.5
  1.3 0.0 copy-done.6
  1.3 0.0 copy-done.7
  1.3 0.0 copy-start
  1.3 1.2 copy-done
  2.5 0.0 copy-start.1
  2.5 0.9 copy-done.1
  3.5 0.0 copy-start.2
  3.5 0.9 copy-done.2
  4.4 0.0 copy-start.3
  4.4 0.9 copy-done.3
  5.3 0.0 copy-start.4
  5.3 0.9 copy-done.4
  6.2 115.9 %shard_map.111 = (bf16[256,132]{1,0:T(8,128)(2,1)S(1)}, bf16[256,256]{1,0:T(8,128)(2,1)S(1)}, bf16[4,2,64,1024]{3,2,1,0:T(8,128)(2,1)S(1)}, f32[176,256]{1,0:T(8,128)S(1)}) custom-call(bf16[256,132]{1,0:T(8,128)(2,1)S(1)} %bitcast.15, bf16[176,256]{1,0:T(8,128)(2,1)S(1)} %bitcast.18, bf16[256,256]{1,0:T(8,128)(2,1)S(1)} %bitcast.16, ...), custom_call_target="tpu_custom_call" | custom-call | tf_op jit(solution)/shard_map/pallas_call | solution.py:412
  122.1 0.7 copy.16
  122.7 0.7 copy.17
  123.4 1.0 copy.18
  124.4 0.7 copy.19
Async XLA Ops:
  0.6 0.7 copy-start.5
  0.6 0.7 copy-start.6
  0.7 0.7 copy-start.7
  1.3 1.2 copy-start
  2.5 0.9 copy-start.1
  3.5 0.9 copy-start.2
  4.4 0.9 copy-start.3
  5.3 0.9 copy-start.4

commit v3 on v2

--- a/solution.py
+++ b/solution.py
@@ -33,9 +33,9 @@
 
 
 def kernel(
-    cot_ref, w_ref, q_ref, kv_hbm, seg_ref, res_ref, live_ref, count_ref,
+    cot_hbm, w_hbm, q_hbm, kv_hbm, seg_hbm, res_hbm, live_ref, count_ref,
     o_res, o_q, o_kv, o_w,
-    c_own, w_own, cg, wg, po, rp, rm, fz, cz, e_send, e_core, es, ex0, ex1, ex2, fe, ez,
+    cot_ref, w_ref, q_ref, seg_ref, res_ref, c_own, w_own, cg, wg, po, rp, rm, fz, cz, e_send, e_core, es, ex0, ex1, ex2, fe, ez,
     d_own, dz, kvs, ctx, bias, probs, dctx,
     ssem, bsem, asem, rpsem, rmsem, czsem, ecsem, exsem, ezsem, dzsem, kvsem, ldsem,
 ):
@@ -78,15 +78,21 @@
             device_id=other, device_id_type=MESH,
         ).wait_recv()
 
+    keys_values = kv_hbm.at[:, :, :, pl.ds(pl.multiple_of(y * HEAD_SIZE, HEAD_SIZE), HEAD_SIZE)]
+    loads = [
+        pltpu.make_async_copy(src, dst, ldsem.at[i])
+        for i, (src, dst) in enumerate((
+            (cot_hbm, cot_ref), (w_hbm, w_ref), (keys_values, kvs),
+            (q_hbm, q_ref), (seg_hbm, seg_ref), (res_hbm, res_ref),
+        ))
+    ]
+    for load in loads:
+        load.start()
+
     partners = [on_y[1], on_y[-1], *on_zl[1:], *on_zh[1:], on_x[1], on_x[-1], other]
     barrier = pltpu.get_barrier_semaphore()
     for partner in partners:
         pl.semaphore_signal(barrier, inc=1, device_id=partner, device_id_type=MESH)
-
-    load = pltpu.make_async_copy(
-        kv_hbm.at[:, :, :, pl.ds(pl.multiple_of(y * HEAD_SIZE, HEAD_SIZE), HEAD_SIZE)], kvs, ldsem
-    )
-    load.start()
 
     units = 0
     for r in range(live_ref.shape[0]):
@@ -94,11 +100,13 @@
     slot = lax.div(lax.broadcasted_iota(jnp.int32, (TOKENS, 1), 0), 64)
     counted = jnp.where(slot < count_ref[dpi], 1, 0) * jnp.where(live_ref[dpi] > 0, 1, 0)
     weight = counted.astype(F32) / jnp.full((TOKENS, 1), jnp.maximum(units, 1), jnp.int32).astype(F32)
+    loads[0].wait()
     scaled = (cot_ref[...].astype(F32) * weight).astype(BF16)
     c_hot = one_hot(C_BLOCKS * ROWS, cot_ref.shape[1])
     c_block = dot(c_hot, scaled, 1, 1).astype(BF16).reshape(C_BLOCKS, ROWS, TOKENS)
     c_own[...] = c_block
     cg[pl.ds(ti * C_BLOCKS, C_BLOCKS)] = c_block
+    loads[1].wait()
     w_block = dot(one_hot(W_BLOCKS * ROWS, w_ref.shape[0]), w_ref[...], 1, 0)
     w_block = w_block.astype(BF16).reshape(W_BLOCKS, ROWS, TOKENS)
     w_own[...] = w_block
@@ -107,8 +115,8 @@
     def c_place(t):
         return cg.at[pl.ds(t * C_BLOCKS, C_BLOCKS)]
 
-    def w_place(d):
-        return wg.at[pl.ds(d * W_BLOCKS, W_BLOCKS)]
+    def w_half(d, h):
+        return wg.at[pl.ds(d * W_BLOCKS + 2 * h, 2)], asem.at[2 * d + h]
 
     scale = 1.0 / math.sqrt(HEAD_SIZE)
 
@@ -156,28 +164,36 @@
             if s < 3 or (s == 3 and mine):
                 send(place(t), place(t), sem.at[t], on_y[k])
 
-    steps = {n: [] for n in range(1, 11)}
+    steps = {n: [] for n in range(1, 12)}
     for s in (4, 3, 2, 1, 0):
         for j in range(4):
             if s + j > 0:
-                steps[s + 2 * j].append((s, j))
+                steps[2 * s + j].append((s, j))
 
     def c_steps(*ns):
         for n in ns:
             for s, j in steps[n]:
                 gather_step(c_place, bsem, s, j)
 
-    def w_x(d_x, zhx, forward):
-        d = (d_x * 3 + zhx) * 2 + core
-        arrive(w_place(d), asem.at[d])
-        if forward:
-            send(w_place(d), w_place(d), asem.at[d], on_x[1])
-        send(w_place(d), w_place(d), asem.at[d], other)
-
-    def w_x_all(zhx):
-        w_x(x_at(-way), zhx, True)
-        w_x(x_at(way), zhx, False)
-        w_x(x_at(2), zhx, False)
+    def w_pass(d, h, *devices):
+        block, sem = w_half(d, h)
+        arrive(block, sem)
+        for device in devices:
+            send(block, block, sem, device)
+
+    def w_from(d_x, zhx):
+        return (d_x * 3 + zhx) * 2 + core
+
+    def w_near(zhx, h):
+        w_pass(w_from(x_at(-way), zhx), h, on_x[1], other)
+        w_pass(w_from(x_at(way), zhx), h, other)
+
+    def w_far(zhx, h):
+        w_pass(w_from(x_at(2), zhx), h, other)
+
+    def w_z(h):
+        for k in (1, 2):
+            w_pass(w_from(x, zhk[k]), h, on_x[1], on_x[-1], other)
 
     def project(i, carry):
         n = 8
@@ -275,43 +291,51 @@
 
     pl.semaphore_wait(barrier, len(partners))
 
-    for k in (1, -1):
-        send(c_own, c_place(ti), bsem.at[ti], on_y[k])
-    send(c_own, c_place(ti), bsem.at[ti], on_zl[1])
-    for k in (1, 2):
-        send(w_own, w_place(dpi), asem.at[dpi], on_zh[k])
-    for k in (1, -1):
-        send(w_own, w_place(dpi), asem.at[dpi], on_x[k])
-    send(w_own, w_place(dpi), asem.at[dpi], other)
-    for j in (2, 3):
-        send(c_own, c_place(ti), bsem.at[ti], on_zl[j])
-
-    load.wait()
+    for device in (on_y[1], on_y[-1], *on_zl[1:]):
+        send(c_own, c_place(ti), bsem.at[ti], device)
+    for h in (0, 1):
+        for device in (on_x[1], on_x[-1], other):
+            send(w_own.at[pl.ds(2 * h, 2)], *w_half(dpi, h), device)
+
+    for load in loads[2:]:
+        load.wait()
     mask()
     attend(0)
     c_steps(1)
     attend(1)
     c_steps(2)
-    w_x_all(zh)
-    c_steps(3, 4)
+    c_steps(3)
+    for h in (0, 1):
+        for device in on_zh[1:]:
+            send(w_own.at[pl.ds(2 * h, 2)], *w_half(dpi, h), device)
+    w_near(zh, 0)
+    w_near(zh, 1)
+    c_steps(4)
+    w_far(zh, 0)
+    w_far(zh, 1)
+    c_steps(5)
+    w_z(0)
+    c_steps(6)
     for k in (1, 2):
-        d = (x * 3 + zhk[k]) * 2 + core
-        arrive(w_place(d), asem.at[d])
-        for m in (1, -1):
-            send(w_place(d), w_place(d), asem.at[d], on_x[m])
-        send(w_place(d), w_place(d), asem.at[d], other)
-    c_steps(5, 6)
-    w_x_all(zhk[1])
-    c_steps(7, 8)
-    w_x_all(zhk[2])
+        w_near(zhk[k], 0)
+    c_steps(7)
+    w_z(1)
+    for k in (1, 2):
+        w_far(zhk[k], 0)
+    c_steps(8)
+    for k in (1, 2):
+        w_near(zhk[k], 1)
+    c_steps(9)
+    for k in (1, 2):
+        w_far(zhk[k], 1)
     for xd in range(4):
         for zd in range(3):
-            d = (xd * 3 + zd) * 2 + 1 - core
-            arrive(w_place(d), asem.at[d])
+            for h in (0, 1):
+                arrive(*w_half((xd * 3 + zd) * 2 + 1 - core, h))
 
     lax.fori_loop(0, BLOCKS // 8, project, 0)
     ring_first()
-    c_steps(9, 10)
+    c_steps(10, 11)
 
     for xd in (x_at(2), x_at(way), x_at(-way), x):
         grad_share(xd)
@@ -407,6 +431,7 @@
     w_shape = (W_BLOCKS, ROWS, TOKENS)
     d_shape = (4, 2, 64, HEAD_SIZE)
     vmem = pl.BlockSpec(memory_space=pltpu.VMEM)
+    hbm = pl.BlockSpec(memory_space=pl.ANY)
     smem = pl.BlockSpec(memory_space=pltpu.SMEM)
     dma = pltpu.SemaphoreType.DMA
     return pl.pallas_call(
@@ -417,9 +442,14 @@
             jax.ShapeDtypeStruct(kv.shape, BF16),
             jax.ShapeDtypeStruct(w.shape, F32),
         ),
-        in_specs=[vmem, vmem, vmem, pl.BlockSpec(memory_space=pl.ANY), vmem, vmem, smem, smem],
+        in_specs=[hbm] * 6 + [smem] * 2,
         out_specs=(vmem, vmem, vmem, vmem),
         scratch_shapes=[
+            pltpu.VMEM(cot.shape, BF16),
+            pltpu.VMEM(w.shape, BF16),
+            pltpu.VMEM(q.shape, BF16),
+            pltpu.VMEM(seg.shape, jnp.int32),
+            pltpu.VMEM(res.shape, BF16),
             pltpu.VMEM(c_shape, BF16),
             pltpu.VMEM(w_shape, BF16),
             pltpu.VMEM((BLOCKS, ROWS, TOKENS), BF16),
@@ -446,7 +476,7 @@
             pltpu.VMEM((TOKENS, TOKENS), F32),
             dma((N_SEND,)),
             dma((32,)),
-            dma((24,)),
+            dma((48,)),
             dma((16,)),
             dma((16,)),
             dma((4,)),
@@ -455,10 +485,10 @@
             dma((3,)),
             dma((4,)),
             dma((32,)),
-            dma(()),
+            dma((6,)),
         ],
         compiler_params=pltpu.CompilerParams(
-            collective_id=0, has_side_effects=True, vmem_limit_bytes=48 * 1024 * 1024
+            collective_id=0, has_side_effects=True, vmem_limit_bytes=60 * 1024 * 1024
         ),
     )(cot, w, q, kv, seg, res, live, counts)
 

time: 125 us -> 101 us (0.81)
  the two profiles are of different devices: /device:TPU:2 before, /device:TPU:1 now
where the time goes in v3:
time: 101 us
  Pallas kernels  95.3 us (94%)
  local copies, waits for them, and re-layouts  5.24 us (5%)
    pallas_call x1, Pallas kernels, exchange(): pl.pallas_call(kernel, out_shape=(jax.ShapeDtypeStruct(res.shape, BF16),...  95.3 us
    unnamed x8, local copies, waits for them, and re-layouts  5.24 us

profile of v3, /device:TPU:1, one launch (start us, length us, event | category | flops | bytes accessed | tf_op | source)
XLA Modules:
  0.0 101.2 jit_solution(4636370545993176240)
XLA Ops:
  0.6 95.3 %shard_map.111 = (bf16[256,132]{1,0:T(8,128)(2,1)}, bf16[256,256]{1,0:T(8,128)(2,1)}, bf16[4,2,64,1024]{3,2,1,0:T(8,128)(2,1)}, f32[176,256]{1,0:T(8,128)}) custom-call(bf16[256,132]{1,0:T(8,128)(2,1)} %bitcast.15, bf16[176,256]{1,0:T(8,128)(2,1)} %bitcast.18, bf16[256,256]{1,0:T(8,128)(2,1)} %bitcast.16, bf16[4,2,64,1024]{3,2,1,0:T(8,128)(2,1)} %bitcast.10, ...), custom_call_target="tpu_custom_call" | custom-call | tf_op jit(solution)/shard_map/pallas_call | solution.py:437
  95.9 0.0 copy-start.1
  96.0 1.6 %copy.16 = bf16[1,4,64,132]{3,2,1,0:T(8,128)(2,1)} copy(bf16[1,4,64,132]{3,2,1,0:T(8,128)(2,1)} %bitcast.14) | data formatting | bytes 135168
  97.6 0.0 copy-done.1
  97.6 0.7 copy.17
  98.2 0.0 copy-start
  98.2 2.3 %copy.18 = bf16[1,4,2,64,1024]{4,3,2,1,0:T(8,128)(2,1)} copy(bf16[1,4,2,64,1024]{4,3,2,1,0:T(8,128)(2,1)} %bitcast.11) | data formatting | bytes 2097152
  100.5 0.0 copy-done
  100.5 0.7 copy.19
Async XLA Ops:
  95.9 1.6 %copy-start.1 = (bf16[256,256]{1,0:T(8,128)(2,1)S(1)}, bf16[256,256]{1,0:T(8,128)(2,1)}, u32[]{:S(2)}) copy-start(bf16[256,256]{1,0:T(8,128)(2,1)} %get-tuple-element.9) | copy-start | bytes 393220
  98.2 2.3 %copy-start = (f32[176,256]{1,0:T(8,128)S(1)}, f32[176,256]{1,0:T(8,128)}, u32[]{:S(2)}) copy-start(f32[176,256]{1,0:T(8,128)} %get-tuple-element.11) | copy-start | bytes 540676

commit v4 on v3

--- a/solution.py
+++ b/solution.py
@@ -201,6 +201,12 @@
         po[pl.ds(i * n, n)] = out.astype(BF16).reshape(n, ROWS, TOKENS)
         return carry
 
+    def w_project(zhx):
+        for d_x in range(4):
+            for h in (0, 1):
+                arrive(*w_half((d_x * 3 + zhx) * 2 + 1 - core, h))
+        lax.fori_loop(0, 4, lambda d_x, carry: project(d_x * 3 + zhx, carry), 0)
+
     recv_buf = {1: (rp, rpsem), -1: (rm, rmsem)}
 
     def p_at(k, j):
@@ -215,17 +221,17 @@
         return (j < 2) if k == 1 else (j >= 2)
 
     def ring_first():
-        for j in range(4):
+        for j in (3, 2, 1, 0):
             for k in (1, -1):
                 if starts(k, j):
                     send(p_at(4, j), *ring_slot(k, 1, j), on_y[k])
-        for j in range(4):
+        for j in (3, 2, 1, 0):
             for k in (1, -1):
                 if not starts(k, j):
                     send(p_at(3 * k, j), *ring_slot(k, 2, j), on_y[k])
 
     def ring_step(r):
-        for j in range(4):
+        for j in (3, 2, 1, 0):
             for k in (1, -1):
                 if r == 1 and not starts(k, j):
                     continue
@@ -297,20 +303,20 @@
         for device in (on_x[1], on_x[-1], other):
             send(w_own.at[pl.ds(2 * h, 2)], *w_half(dpi, h), device)
 
-    for load in loads[2:]:
-        load.wait()
-    mask()
-    attend(0)
     c_steps(1)
-    attend(1)
     c_steps(2)
     c_steps(3)
     for h in (0, 1):
         for device in on_zh[1:]:
             send(w_own.at[pl.ds(2 * h, 2)], *w_half(dpi, h), device)
+    for load in loads[2:]:
+        load.wait()
+    mask()
+    attend(0)
     w_near(zh, 0)
     w_near(zh, 1)
     c_steps(4)
+    attend(1)
     w_far(zh, 0)
     w_far(zh, 1)
     c_steps(5)
@@ -323,17 +329,14 @@
     for k in (1, 2):
         w_far(zhk[k], 0)
     c_steps(8)
+    w_project(zh)
     for k in (1, 2):
         w_near(zhk[k], 1)
     c_steps(9)
     for k in (1, 2):
         w_far(zhk[k], 1)
-    for xd in range(4):
-        for zd in range(3):
-            for h in (0, 1):
-                arrive(*w_half((xd * 3 + zd) * 2 + 1 - core, h))
-
-    lax.fori_loop(0, BLOCKS // 8, project, 0)
+    for k in (1, 2):
+        w_project(zhk[k])
     ring_first()
     c_steps(10, 11)
 
@@ -391,7 +394,7 @@
         fe[k] = arrived(zhk[k]).astype(BF16)
         send(fe.at[k], ez.at[k], ezsem.at[k], on_zh[k])
 
-    for j in (1, 2, 3):
+    for j in (3, 2, 1):
         fz[j] = ring_last(j).astype(BF16)
         send(fz.at[j], cz.at[j], czsem.at[j], on_zl[j])
 

time: 101 us -> 99.5 us (0.985); the launches traced: 101 us -> 98 us
  Pallas kernels: 95.3 us -> 92.2 us
    pallas_call x1, Pallas kernels: 95.3 us -> 92.2 us  [exchange(): pl.pallas_call(kernel, out_shape=(jax.ShapeDtypeStruct(res.shape, BF16),...]
where the time goes in v4:
time: 99.5 us; the launch traced here: 98 us
  Pallas kernels  92.2 us (93%)
  local copies, waits for them, and re-layouts  5.24 us (5%)
    pallas_call x1, Pallas kernels, exchange(): pl.pallas_call(kernel, out_shape=(jax.ShapeDtypeStruct(res.shape, BF16),...  92.2 us
    unnamed x8, local copies, waits for them, and re-layouts  5.24 us

profile of v4, /device:TPU:1, one launch (start us, length us, event | category | flops | bytes accessed | tf_op | source)
XLA Modules:
  0.0 98.0 jit_solution(15318010474186573851)
XLA Ops:
  0.6 92.2 %shard_map.111 = (bf16[256,132]{1,0:T(8,128)(2,1)}, bf16[256,256]{1,0:T(8,128)(2,1)}, bf16[4,2,64,1024]{3,2,1,0:T(8,128)(2,1)}, f32[176,256]{1,0:T(8,128)}) custom-call(bf16[256,132]{1,0:T(8,128)(2,1)} %bitcast.15, bf16[176,256]{1,0:T(8,128)(2,1)} %bitcast.18, bf16[256,256]{1,0:T(8,128)(2,1)} %bitcast.16, bf16[4,2,64,1024]{3,2,1,0:T(8,128)(2,1)} %bitcast.10, ...), custom_call_target="tpu_custom_call" | custom-call | tf_op jit(solution)/shard_map/pallas_call | solution.py:440
  92.8 0.0 copy-start.1
  92.8 1.6 %copy.16 = bf16[1,4,64,132]{3,2,1,0:T(8,128)(2,1)} copy(bf16[1,4,64,132]{3,2,1,0:T(8,128)(2,1)} %bitcast.14) | data formatting | bytes 135168
  94.4 0.0 copy-done.1
  94.4 0.7 copy.17
  95.1 0.0 copy-start
  95.1 2.3 %copy.18 = bf16[1,4,2,64,1024]{4,3,2,1,0:T(8,128)(2,1)} copy(bf16[1,4,2,64,1024]{4,3,2,1,0:T(8,128)(2,1)} %bitcast.11) | data formatting | bytes 2097152
  97.4 0.0 copy-done
  97.4 0.7 copy.19
Async XLA Ops:
  92.8 1.6 %copy-start.1 = (bf16[256,256]{1,0:T(8,128)(2,1)S(1)}, bf16[256,256]{1,0:T(8,128)(2,1)}, u32[]{:S(2)}) copy-start(bf16[256,256]{1,0:T(8,128)(2,1)} %get-tuple-element.9) | copy-start | bytes 393220
  95.1 2.3 %copy-start = (f32[176,256]{1,0:T(8,128)S(1)}, f32[176,256]{1,0:T(8,128)}, u32[]{:S(2)}) copy-start(f32[176,256]{1,0:T(8,128)} %get-tuple-element.11) | copy-start | bytes 540676
